TPU v7x, 256 devices: a whole 4x4x8 slice. The times are simulated.
256 devices in a mesh: ctx: 8 (over x, y_hi), mp: 32 (over y_lo, z, core).
Axes of the slice: x: 4, y: 4 (y_hi: 2, y_lo: 2; y = y_hi * 2 + y_lo), z: 8, core: 2. Of those that a mesh axis runs over, the one named last changes fastest.
Arguments:
- hidden_states: bfloat16 [24576, 8192], P('ctx', 'mp'), may hold values from -8 to 8
- route_slot: int32 [4608], P('ctx'), may hold values from 0 to 3071, as said below
- route_live: int32 [4608], P('ctx'), may hold values from 0 to 1, as said below
- router_weight: bfloat16 [8192], replicated, may hold values from -0.0625 to 0.0625
- query_weight: bfloat16 [8192, 8192], P(None, 'mp')
- keyval_weight: bfloat16 [8192, 2048], P(None, 'mp')
- output_weight: bfloat16 [8192, 8192], P('mp'), may hold values from -0.75 to 0.75
Outputs:
- mixed_states: bfloat16 [24576, 8192], P('ctx', 'mp')
Inputs may be any that keep to these rules, and one draw needn't show every extreme that they name: `route_slot`: within each owner's 576 slots the live slots come first and hold distinct ascending offsets below 3072; dead slots hold 0. The last token of every owner is routed. `route_live`: each owner has from 192 to 576 live slots, all at its first slots; together they are exactly 3072; some owner has all 576 live.
All inputs are finite; a program needn't handle non-finite values.
Results may differ from a plain program's by a relative error of at most 0.03.
Values may be sent and summed in bfloat16 or wider, within the bound.
No kernel may reach another device: no remote copies, remote signals or barrier semaphores. Data moves between devices by JAX's collectives and lax.ppermute only.
A program may use at most 128 MiB of HBM per device.

v0:
```python
import jax
import jax.numpy as jnp
from jax import lax
from jax.sharding import PartitionSpec as P

GROUP = 8
HQ_DEV = 2


far_position = 1073741824


def partner_2(value, axis, apart):
    return lax.ppermute(value, axis, [(i, i ^ 1 << apart) for i in range(lax.axis_size(axis))])


def attend_block(state_tuple, queries, query_pos, keyval_rows, key_pos):
    running_max, running_sum, weighted = state_tuple
    width = queries.shape[1]
    key_part = keyval_rows[:, :width]
    value_part = keyval_rows[:, width:]
    scores = lax.dot_general(
        queries, key_part, (((1,), (1,)), ((), ())), preferred_element_type=jnp.float32
    ) * width ** (-0.5)
    allowed = key_pos[None, :] <= query_pos[:, None]
    masked = jnp.where(allowed, scores, -1e30)
    new_max = jnp.maximum(running_max, jnp.max(masked, axis=1))
    weights = jnp.where(allowed, jnp.exp(masked - new_max[:, None]), 0.0)
    shrink = jnp.exp(running_max - new_max)
    running_sum = running_sum * shrink + jnp.sum(weights, axis=1)
    weighted = weighted * shrink[:, None] + jnp.dot(
        weights.astype(jnp.bfloat16), value_part, preferred_element_type=jnp.float32
    )
    return (new_max, running_sum, weighted)


def routed_update(
    routed_rows, positions, router_weight, query_weight, keyval_weight, output_weight
):
    row_total = routed_rows.shape[0]
    local_width = query_weight.shape[1]
    head_width = keyval_weight.shape[1] * GROUP // (2 * HQ_DEV)
    head_count = local_width // head_width
    fragment = lax.all_gather(routed_rows, "mp", axis=1, tiled=True)
    keyval_rows = keyval_weight
    query_acc = jnp.dot(fragment, query_weight, preferred_element_type=jnp.float32)
    keyval_acc = jnp.dot(fragment, keyval_rows, preferred_element_type=jnp.float32)
    logit_acc = jnp.dot(fragment, router_weight, preferred_element_type=jnp.float32)
    query_acc, keyval_acc, logit_acc = (query_acc, keyval_acc, logit_acc)
    queries = query_acc.astype(jnp.bfloat16)
    stacked_queries = (
        queries.reshape(row_total, head_count, head_width)
        .transpose(1, 0, 2)
        .reshape(head_count * row_total, head_width)
    )
    stacked_pos = jnp.tile(positions, head_count)
    own_keyval = keyval_acc.astype(jnp.bfloat16)
    mp_index = lax.axis_index("mp")
    bit_count = (GROUP // HQ_DEV).bit_length() - 1
    for bit_number in range(bit_count):
        partner = partner_2(own_keyval, "mp", bit_number)
        upper_side = mp_index >> bit_number & 1 == 1
        own_keyval = jnp.where(
            upper_side,
            jnp.concatenate([partner, own_keyval], axis=1),
            jnp.concatenate([own_keyval, partner], axis=1),
        )
    stacked_rows = head_count * row_total
    start_state = (
        jnp.full((stacked_rows,), -1e30, jnp.float32),
        jnp.zeros((stacked_rows,), jnp.float32),
        jnp.zeros((stacked_rows, head_width), jnp.float32),
    )
    state_tuple = start_state
    keyval_rows = lax.all_gather(own_keyval, "ctx", axis=0, tiled=True)
    key_pos = lax.all_gather(positions, "ctx", axis=0, tiled=True)
    amount = keyval_rows.shape[0]
    blocks = amount // 512

    def step_block(inner, item):
        return (attend_block(inner, stacked_queries, stacked_pos, item[0], item[1]), None)

    stacked = (keyval_rows.reshape(blocks, 512, keyval_rows.shape[1]), key_pos.reshape(blocks, 512))
    state_tuple, unused = lax.scan(step_block, state_tuple, stacked)
    running_max, running_sum, weighted = state_tuple
    stacked_attended = (weighted / running_sum[:, None]).astype(jnp.bfloat16)
    attended = (
        stacked_attended.reshape(head_count, row_total, head_width)
        .transpose(1, 0, 2)
        .reshape(row_total, local_width)
    )
    gate_value = jax.nn.sigmoid(logit_acc)
    combined = lax.psum_scatter(
        lax.dot_general(
            output_weight, attended, (((0,), (1,)), ((), ())), preferred_element_type=jnp.float32
        ).astype(jnp.bfloat16),
        "mp",
        scatter_dimension=0,
        tiled=True,
    ).astype(jnp.float32)
    return (gate_value[:, None] * combined.T).astype(jnp.bfloat16)


def local(
    hidden_states, route_slot, route_live, router_weight, query_weight, keyval_weight, output_weight
):
    seq_dev = hidden_states.shape[0]
    ctx_id = lax.axis_index("ctx")
    own_rows = jnp.take(hidden_states, route_slot, axis=0)
    positions = jnp.where(route_live == 1, ctx_id * seq_dev + route_slot, far_position)
    update = routed_update(
        own_rows, positions, router_weight, query_weight, keyval_weight, output_weight
    )
    addition = jnp.where(route_live[:, None] == 1, update.astype(jnp.float32), 0.0)
    widened = hidden_states.astype(jnp.float32).at[route_slot].add(addition)
    return widened.astype(jnp.bfloat16)


def solution(mesh):
    placed = (P("ctx", "mp"), P("ctx"), P("ctx"), P(), P(None, "mp"), P(None, "mp"), P("mp", None))
    return jax.shard_map(
        local, mesh=mesh, in_specs=placed, out_specs=P("ctx", "mp"), check_vma=False
    )
```

profile of v0, /device:TPU:8, one launch (start us, length us, event | category | flops | bytes accessed | tf_op | source)
XLA Modules:
  0.0 373.3 jit_solution(8200890812531677743)
XLA Ops:
  6.5 0.8 compare_and_fusion
  7.3 1.3 dynamic-slice
  9.2 0.8 fusion.25
  10.1 3.8 %gather_fusion = bf16[576,256]{1,0:T(8,128)(2,1)S(1)} fusion(bf16[3072,256]{1,0:T(8,128)(2,1)} %param.9, s32[1024]{0:T(1024)S(1)} %pad_clamp_fusion), kind=kCustom, calls=%fused_computation | custom fusion | bytes 592128 | tf_op jit(solution)/shard_map/jit(_take)/gather | solution.py:109
  13.9 0.9 broadcast_select_fusion
  14.8 97.5 %all-gather.3.cloned.1.call-done = bf16[576,8192]{1,0:T(8,128)(2,1)} async-done(((bf16[576,256]{1,0:T(8,128)(2,1)}), bf16[576,8192]{1,0:T(8,128)(2,1)}) %all-gather.3.cloned.1.call-update) | async-done | bytes 9437200 | tf_op jit(solution)/shard_map/all_gather | solution.py:44
  112.3 6.6 %convolution_convert_fusion.2 = bf16[576,64]{0,1:T(8,128)(2,1)S(1)} fusion(bf16[576,8192]{1,0:T(8,128)(2,1)} %all-gather.3.cloned.1.call-done, bf16[8192,64]{0,1:T(8,128)(2,1)S(1)} %copy-done), kind=kOutput, calls=%fused_computation.27 | convolution fusion | flops 604016640 | bytes 10559488 | tf_op jit(solution)/shard_map/dot_general | solution.py:47
  118.9 0.3 collective-permute-start
  119.3 1.0 collective-permute-done
  120.3 0.1 collective-permute-start.1
  120.4 6.3 %collective-permute-done.1 = bf16[576,128]{0,1:T(8,128)(2,1)S(1)} collective-permute-done((bf16[576,128]{0,1:T(8,128)(2,1)S(1)}, bf16[576,128]{0,1:T(8,128)(2,1)S(1)}, u32[]{:S(2)}, u32[]{:S(2)}) %collective-permute-start.1) | collective-permute-done | bytes 147488 | tf_op jit(solution)/shard_map/ppermute | solution.py:14
  126.9 0.9 copy.13
  127.8 41.0 %all-reduce = s32[4608]{0:T(1024)S(1)} all-reduce(s32[4608]{0:T(1024)S(1)} %get-tuple-element.106), channel_id=1, replica_groups=mesh['ctx'=8,'mp'=32] {'ctx'}, use_global_device_ids=true, to_apply=%add | all-reduce | flops 4608 | bytes 36864
  168.9 7.5 %convolution_convert_fusion.1 = bf16[576,256]{1,0:T(8,128)(2,1)S(1)} fusion(bf16[576,8192]{1,0:T(8,128)(2,1)} %all-gather.3.cloned.1.call-done, bf16[8192,256]{1,0:T(8,128)(2,1)} %param.13), kind=kOutput, calls=%fused_computation.26 | convolution fusion | flops 2416066560 | bytes 13926400 | tf_op jit(solution)/shard_map/dot_general | solution.py:46
  176.5 11.3 %all-gather.5.cloned.1.call-done = bf16[4608,256]{1,0:T(8,128)(2,1)} async-done(((bf16[576,256]{1,0:T(8,128)(2,1)}), bf16[4608,256]{1,0:T(8,128)(2,1)}) %all-gather.5.cloned.1.call-update) | async-done | bytes 2359312 | tf_op jit(solution)/shard_map/all_gather | solution.py:75
  187.8 27.0 %while.15 = (s32[]{:T(128)}, f32[1152]{0:T(1024)S(1)}, f32[1152]{0:T(1024)S(1)}, f32[1152,128]{1,0:T(8,128)S(1)}, s32[9,512]{1,0:T(8,128)S(1)}, /*index=5*/bf16[...) while((s32[]{:T(128)}, f32[1152]{0:T(1024)S(1)}, ...), condition=%wide.region_3.4_spmd.clone, body=%wide.region_0.3_spmd.clone.sunk | while | flops 309515904 | bytes 9467265 | solution.py:84
  187.9 0.1 le.67
  187.9 1.0 dynamic-slice_bitcast_fusion.2
  188.9 0.5 fusion.44
  189.4 0.5 fusion.45
  190.0 0.8 convolution_add_fusion.2
  190.9 0.1 le.67
  190.9 1.0 dynamic-slice_bitcast_fusion.2
  191.9 0.5 fusion.44
  192.5 0.5 fusion.45
  193.0 0.8 convolution_add_fusion.2
  193.9 0.1 le.67
  193.9 1.0 dynamic-slice_bitcast_fusion.2
  194.9 0.5 fusion.44
  195.5 0.5 fusion.45
  196.0 0.8 convolution_add_fusion.2
  197.0 1.0 dynamic-slice_bitcast_fusion.2
  197.9 0.5 fusion.44
  198.5 0.5 fusion.45
  199.0 0.8 convolution_add_fusion.2
  200.0 1.0 dynamic-slice_bitcast_fusion.2
  200.9 0.5 fusion.44
  201.5 0.5 fusion.45
  202.0 0.8 convolution_add_fusion.2
  203.0 1.0 dynamic-slice_bitcast_fusion.2
  203.9 0.5 fusion.44
  204.5 0.5 fusion.45
  205.0 0.8 convolution_add_fusion.2
  206.0 1.0 dynamic-slice_bitcast_fusion.2
  206.9 0.5 fusion.44
  207.5 0.5 fusion.45
  208.0 0.8 convolution_add_fusion.2
  209.0 1.0 dynamic-slice_bitcast_fusion.2
  209.9 0.5 fusion.44
  210.5 0.5 fusion.45
  211.0 0.8 convolution_add_fusion.2
  212.0 1.0 dynamic-slice_bitcast_fusion.2
  213.0 0.5 fusion.44
  213.5 0.5 fusion.45
  214.0 0.8 convolution_add_fusion.2
  214.9 0.2 divide_convert_fusion
  215.1 0.3 copy.15
  215.4 7.3 %fusion.15 = bf16[8192,576]{0,1:T(8,128)(2,1)} fusion(bf16[256,8192]{1,0:T(8,128)(2,1)} %param.15, bf16[72,8,2,128]{3,2,1,0:T(2,128)(2,1)S(1)} %bitcast.36), kind=kOutput, calls=%fused_computation.25 | convolution fusion | flops 2420637696 | bytes 13926400 | tf_op jit(solution)/shard_map/dot_general | solution.py:94
  222.7 1.4 copy-done.1
  224.1 1.9 convert_element_type.35
  226.0 6.2 %convolution_reduce_fusion = f32[576]{0:T(1024)S(1)} fusion(bf16[576,8192]{1,0:T(8,128)(2,1)} %all-gather.3.cloned.1.call-done, bf16[8192,1]{0,1:T(2,128)(2,1)S(1)} %reshape.60), kind=kOutput, calls=%fused_computation.28 | convolution fusion | flops 9437184 | bytes 9455872 | tf_op jit(solution)/shard_map/dot_general | solution.py:48
  232.3 120.6 %reduce-scatter.2.cloned.1.call-done = bf16[256,576]{0,1:T(8,128)(2,1)} async-done(((bf16[8192,576]{0,1:T(8,128)(2,1)}), bf16[256,576]{0,1:T(8,128)(2,1)}) %reduce-scatter.2.cloned.1.call-update) | async-done | bytes 294928 | tf_op jit(solution)/shard_map/reduce_scatter | solution.py:93
  352.9 10.7 %scatter_custom_fusion = f32[3072,256]{1,0:T(8,128)} fusion(f32[3072,256]{1,0:T(8,128)} %convert_element_type.35, s32[576]{0:T(1024)S(1)} %get-tuple-element.111, bf16[256,576]{0,1:T(8,128)(2,1)} %reduce-scatter.2.cloned.1.call-done, f32[]{:T(128)} %constant.33.clone.1, f32[576]{0:T(1024)S(1)} %add_divide_fusion, pred[576]{0:T(1024)(128)(4,1)S(1)} %get-tuple-element.108), kind=kCustom, calls=%fused_computation.29 | custom fusion | flops 884736 | bytes 3446272 | tf_op jit(solution)/shard_map/scatter-add | solution.py:115
  363.6 3.2 convert_element_type.44
  (74 shorter events, 1.2 us)
Async XLA Ops:
  6.5 105.8 %copy-start = (bf16[8192,64]{0,1:T(8,128)(2,1)S(1)}, bf16[8192,64]{0,1:T(8,128)(2,1)}, u32[]{:S(2)}) copy-start(bf16[8192,64]{0,1:T(8,128)(2,1)} %param.14) | copy-start | bytes 3145732
  6.5 105.8 %all-gather.3.cloned.1.call-start = ((), (), s32[]{:S(2)}) async-start(), calls=%async_computation.1 | async-start | bytes 9732096 | tf_op jit(solution)/shard_map/all_gather | solution.py:44
  14.7 173.1 %all-gather.5.cloned.1.call-start = ((), (), s32[]{:S(2)}) async-start(), calls=%async_computation.2 | async-start | bytes 2654208 | tf_op jit(solution)/shard_map/all_gather | solution.py:75
  118.9 1.4 collective-permute-start
  120.3 6.4 %collective-permute-start.1 = (bf16[576,128]{0,1:T(8,128)(2,1)S(1)}, bf16[576,128]{0,1:T(8,128)(2,1)S(1)}, u32[]{:S(2)}, u32[]{:S(2)}) collective-permute-start(bf16[576,128]{0,1:T(8,128)(2,1)S(1)} %maximum_select_fusion.1), channel_id=1, source_target_pairs={{0,2},{1,3},{2,0},{3,1},{4,6},{5,7},{6,4},{7,5},{8,10},{9,11},{10,... | collective-permute-start | bytes 442376 | tf_op jit(solution)/shard_map/ppermute | solution.py:14
  127.8 225.2 %reduce-scatter.2.cloned.1.call-start = ((), (), s32[]{:S(2)}) async-start(), calls=%async_computation.3 | async-start | bytes 9732096 | tf_op jit(solution)/shard_map/reduce_scatter | solution.py:93
  222.7 1.4 copy-start.1
  224.1 1.9 copy-start.2
Sparse Core Ops, SparseCore 0:
  14.9 97.4 all-gather.2
  127.9 59.9 all-gather.4
  222.8 130.0 reduce-scatter.1
where the time goes:
time: 375 us; the launch traced here: 373 us
  waiting for transfers between devices  237 us (63%)
  blocking collectives  41 us (11%)
  matrix products  39.8 us (11%)
  other arithmetic  23.2 us (6%)
  local copies, waits for them, and re-layouts  17.3 us (5%)
  between operations  13.9 us (4%)
    reduce_scatter x1, waiting for transfers between devices, routed_update(): lax.psum_scatter(lax.dot_general(output_weight, attended, (((0,), (1,)),...  121 us
    all_gather x1, waiting for transfers between devices, routed_update(): fragment = lax.all_gather(routed_rows, 'mp', axis=1, tiled=True)  97.5 us
    unnamed x1, blocking collectives  41 us
    all_gather x1, waiting for transfers between devices, routed_update(): keyval_rows = lax.all_gather(own_keyval, 'ctx', axis=0, tiled=True)  11.3 us
    scatter-add x1, other arithmetic, local(): widened = hidden_states.astype(jnp.float32).at[route_slot].add(addition)  10.7 us
    squeeze x9, local copies, waits for them, and re-layouts, routed_update(): state_tuple, unused = lax.scan(step_block, state_tuple, stacked)  8.71 us
    dot_general x9, matrix products, attend_block(): jnp.dot(weights.astype(jnp.bfloat16), value_part, preferred_element_type=...  7.55 us
  transfers between devices with their start and end apart: 5, of which 5 were waited for; matrix products, arithmetic and copies ran while one was open for 4% of the time, Pallas kernels for 0%

commit v1 on v0

v1 whole, which is shorter than its diff:
```python
import functools

import jax
import jax.numpy as jnp
from jax import lax
from jax.experimental import pallas as pl
from jax.experimental.pallas import tpu as pltpu
from jax.sharding import PartitionSpec as P

BF = jnp.bfloat16
F32 = jnp.float32
CTX = 8
NY, NZ, NC = 2, 8, 2
HEAD = 128
WIDTH = 256
FAR = 1 << 29
VMEM_LIMIT = 50 * 1024 * 1024


def mp_perm(move):
    pairs = []
    for i in range(NY * NZ * NC):
        y, z, c = i // (NZ * NC), (i // NC) % NZ, i % NC
        y, z, c = move(y, z, c)
        pairs.append((i, (y * NZ + z) * NC + c))
    return pairs


UP = mp_perm(lambda y, z, c: (y, (z + 1) % NZ, c))
DOWN = mp_perm(lambda y, z, c: (y, (z - 1) % NZ, c))
ACROSS = mp_perm(lambda y, z, c: (1 - y, z, c))
SIBLING = mp_perm(lambda y, z, c: (y, z, 1 - c))
PARTNER = mp_perm(lambda y, z, c: (y, z ^ 1, c))


def send(value, pairs):
    return lax.ppermute(value, "mp", pairs)


def params(**more):
    return pltpu.CompilerParams(vmem_limit_bytes=VMEM_LIMIT, **more)


def gather_kernel(slot_ref, hidden_ref, first_ref, second_ref):
    rows = slot_ref.shape[1]
    tokens = hidden_ref.shape[0]
    spread = jnp.transpose(jnp.broadcast_to(slot_ref[...], (128, rows)))
    lane = lax.broadcasted_iota(jnp.int32, (rows, 128), 1)
    total = jnp.zeros((rows, WIDTH), F32)
    for step in range(tokens // 256):
        parts = [
            (spread == lane + (step * 256 + part * 128)).astype(F32).astype(BF) for part in range(2)
        ]
        total += jnp.dot(
            jnp.concatenate(parts, axis=1),
            hidden_ref[step * 256 : (step + 1) * 256, :],
            preferred_element_type=F32,
        )
    cut = first_ref.shape[0]
    first_ref[...] = total[:cut].astype(BF)
    second_ref[...] = total[cut:].astype(BF)


def gather_rows(hidden, slot, cut):
    rows = slot.shape[0]
    return pl.pallas_call(
        gather_kernel,
        out_shape=(
            jax.ShapeDtypeStruct((cut, WIDTH), BF),
            jax.ShapeDtypeStruct((rows - cut, WIDTH), BF),
        ),
        compiler_params=params(),
        cost_estimate=pl.CostEstimate(
            flops=2 * rows * hidden.shape[0] * WIDTH, bytes_accessed=2_500_000, transcendentals=0
        ),
    )(slot.reshape(1, rows), hidden)


def scatter_kernel(slot_ref, gate_ref, first_ref, second_ref, hidden_ref, out_ref):
    rows = slot_ref.shape[1]
    combined = jnp.concatenate([first_ref[...], second_ref[...]], axis=0)
    update = (jax.nn.sigmoid(gate_ref[:, 0:1]) * combined).astype(BF)
    tile = hidden_ref.shape[0]
    token = lax.broadcasted_iota(jnp.int32, (tile, rows), 0) + pl.program_id(0) * tile
    chosen = (token == slot_ref[...]).astype(F32).astype(BF)
    addition = jnp.dot(chosen, update, preferred_element_type=F32)
    out_ref[...] = (hidden_ref[...].astype(F32) + addition).astype(BF)


def scatter_rows(hidden, slot, logit, first, second):
    tokens = hidden.shape[0]
    rows = slot.shape[0]
    tile = 512
    whole = lambda shape: pl.BlockSpec(shape, lambda i: (0, 0))
    return pl.pallas_call(
        scatter_kernel,
        grid=(tokens // tile,),
        in_specs=[
            whole((1, rows)),
            whole(logit.shape),
            whole(first.shape),
            whole(second.shape),
            pl.BlockSpec((tile, WIDTH), lambda i: (i, 0)),
        ],
        out_specs=pl.BlockSpec((tile, WIDTH), lambda i: (i, 0)),
        out_shape=jax.ShapeDtypeStruct((tokens, WIDTH), BF),
        compiler_params=params(),
        cost_estimate=pl.CostEstimate(
            flops=2 * rows * tokens * WIDTH, bytes_accessed=4_000_000, transcendentals=0
        ),
    )(slot.reshape(1, rows), logit, first, second, hidden)


def halves_kernel(place_ref, query_ref, keyval_ref, output_ref, q_ref, kv_ref, o_ref):
    q_ref[...] = query_ref[...]
    kv_ref[...] = keyval_ref[...]
    o_ref[...] = output_ref[...]


def sibling_halves(place, query_weight, keyval_t, output_weight):
    count = NY * NZ
    return pl.pallas_call(
        halves_kernel,
        grid_spec=pltpu.PrefetchScalarGridSpec(
            num_scalar_prefetch=1,
            grid=(count,),
            in_specs=[
                pl.BlockSpec((WIDTH, WIDTH), lambda i, p: (2 * i + 1 - p[2], 0)),
                pl.BlockSpec((64, WIDTH), lambda i, p: (0, 2 * i + 1 - p[2])),
                pl.BlockSpec((WIDTH, WIDTH), lambda i, p: (0, 2 * i + 1 - p[2])),
            ],
            out_specs=[
                pl.BlockSpec((WIDTH, WIDTH), lambda i, p: (i, 0)),
                pl.BlockSpec((64, WIDTH), lambda i, p: (0, i)),
                pl.BlockSpec((WIDTH, WIDTH), lambda i, p: (0, i)),
            ],
        ),
        out_shape=(
            jax.ShapeDtypeStruct((count * WIDTH, WIDTH), BF),
            jax.ShapeDtypeStruct((64, count * WIDTH), BF),
            jax.ShapeDtypeStruct((WIDTH, count * WIDTH), BF),
        ),
        compiler_params=params(),
        cost_estimate=pl.CostEstimate(flops=0, bytes_accessed=9_000_000, transcendentals=0),
    )(place, query_weight, keyval_t, output_weight)


def project_weight_kernel(
    place_ref, q0, q1, sq0, sq1, kv0, kv1, skv0, skv1, r0, r1, out_ref
):
    core = place_ref[2]
    for part, (own_q, sib_q, own_kv, sib_kv, router) in enumerate(
        ((q0, sq0, kv0, skv0, r0), (q1, sq1, kv1, skv1, r1))
    ):
        rows = slice(part * WIDTH, (part + 1) * WIDTH)
        out_ref[0, rows, 0:256] = own_q[...]
        out_ref[0, rows, 256:512] = sib_q[...]
        mine, theirs = own_kv[...].astype(F32), sib_kv[...].astype(F32)
        low = jnp.where(core == 0, mine, theirs)
        high = jnp.where(core == 0, theirs, mine)
        out_ref[0, rows, 512:640] = jnp.transpose(jnp.concatenate([low, high], axis=0)).astype(BF)
        spread = jnp.broadcast_to(router[0].astype(F32), (128, WIDTH))
        out_ref[0, rows, 640:768] = jnp.transpose(spread).astype(BF)


def project_weights(place, query_weight, sib_query, keyval_t, sib_keyval_t, router_weight):
    def both(shape, index):
        return [
            pl.BlockSpec(shape, functools.partial(index, 0)),
            pl.BlockSpec(shape, functools.partial(index, 1)),
        ]

    def spot(part, i, p):
        y = jnp.where(part == 0, p[0], 1 - p[0])
        return y * NZ + lax.rem(p[1] + i, NZ)

    specs = (
        both((WIDTH, WIDTH), lambda part, i, p: (2 * spot(part, i, p) + p[2], 0))
        + both((WIDTH, WIDTH), lambda part, i, p: (spot(part, i, p), 0))
        + both((64, WIDTH), lambda part, i, p: (0, 2 * spot(part, i, p) + p[2]))
        + both((64, WIDTH), lambda part, i, p: (0, spot(part, i, p)))
        + both((1, 1, WIDTH), lambda part, i, p: (2 * spot(part, i, p) + p[2], 0, 0))
    )
    router = router_weight.reshape(NY * NZ * NC, 1, WIDTH)
    return pl.pallas_call(
        project_weight_kernel,
        grid_spec=pltpu.PrefetchScalarGridSpec(
            num_scalar_prefetch=1,
            grid=(NZ,),
            in_specs=specs,
            out_specs=pl.BlockSpec((1, 512, 768), lambda i, p: (i, 0, 0)),
        ),
        out_shape=jax.ShapeDtypeStruct((NZ, 512, 768), BF),
        compiler_params=params(),
        cost_estimate=pl.CostEstimate(flops=0, bytes_accessed=12_000_000, transcendentals=0),
    )(
        place, query_weight, query_weight, sib_query, sib_query, keyval_t, keyval_t,
        sib_keyval_t, sib_keyval_t, router, router,
    )


def output_weight_kernel(place_ref, o0, o1, so0, so1, out_ref):
    out_ref[0, 0:256, 0:256] = o0[...]
    out_ref[0, 0:256, 256:512] = o1[...]
    out_ref[0, 256:512, 0:256] = so0[...]
    out_ref[0, 256:512, 256:512] = so1[...]


def output_weights(place, output_weight, sib_output):
    def spot(part, i, p):
        y = p[0] if part == 0 else 1 - p[0]
        return y * NZ + lax.rem(p[1] + i, NZ)

    block = (WIDTH, WIDTH)
    return pl.pallas_call(
        output_weight_kernel,
        grid_spec=pltpu.PrefetchScalarGridSpec(
            num_scalar_prefetch=1,
            grid=(NZ,),
            in_specs=[
                pl.BlockSpec(block, lambda i, p: (0, 2 * spot(0, i, p) + p[2])),
                pl.BlockSpec(block, lambda i, p: (0, 2 * spot(1, i, p) + p[2])),
                pl.BlockSpec(block, lambda i, p: (0, spot(0, i, p))),
                pl.BlockSpec(block, lambda i, p: (0, spot(1, i, p))),
            ],
            out_specs=pl.BlockSpec((1, 512, 512), lambda i, p: (i, 0, 0)),
        ),
        out_shape=jax.ShapeDtypeStruct((NZ, 512, 512), BF),
        compiler_params=params(),
        cost_estimate=pl.CostEstimate(flops=0, bytes_accessed=8_000_000, transcendentals=0),
    )(place, output_weight, output_weight, sib_output, sib_output)


def attend_kernel(rank_ref, query_ref, *refs):
    pieces = (len(refs) - 1) // 2
    keyvals, key_ranks, out_ref = refs[:pieces], refs[pieces : 2 * pieces], refs[-1]
    scale = HEAD ** (-0.5)
    own_rank = rank_ref[:, 0:1]
    masked = []
    for keyval, key_rank in zip(keyvals, key_ranks):
        scores = lax.dot_general(
            query_ref[...],
            keyval[:, 0:HEAD],
            (((1,), (1,)), ((), ())),
            preferred_element_type=F32,
        )
        masked.append(jnp.where(key_rank[...] <= own_rank, scores * scale, -1e30))
    top = functools.reduce(
        jnp.maximum, [jnp.max(part, axis=1, keepdims=True) for part in masked]
    )
    total = jnp.zeros_like(top)
    result = jnp.zeros((query_ref.shape[0], HEAD), F32)
    for keyval, part in zip(keyvals, masked):
        weights = jnp.exp(part - top)
        total += jnp.sum(weights, axis=1, keepdims=True)
        result += jnp.dot(weights.astype(BF), keyval[:, HEAD:], preferred_element_type=F32)
    out_ref[...] = (result / total).astype(BF)


def attend(query_rank, queries, keyvals, key_ranks, tile):
    rows = queries.shape[0]
    keys = sum(piece.shape[0] for piece in keyvals)
    whole = lambda piece: pl.BlockSpec(piece.shape, lambda i, h: (0, 0))
    return pl.pallas_call(
        attend_kernel,
        grid=(rows // tile, queries.shape[1] // HEAD),
        in_specs=[
            pl.BlockSpec((tile, 128), lambda i, h: (i, 0)),
            pl.BlockSpec((tile, HEAD), lambda i, h: (i, h)),
            *[whole(piece) for piece in keyvals],
            *[whole(piece) for piece in key_ranks],
        ],
        out_specs=pl.BlockSpec((tile, HEAD), lambda i, h: (i, h)),
        out_shape=jax.ShapeDtypeStruct(queries.shape, BF),
        compiler_params=params(),
        cost_estimate=pl.CostEstimate(
            flops=8 * rows * keys * HEAD, bytes_accessed=4_000_000, transcendentals=2 * rows * keys
        ),
    )(query_rank, queries, *keyvals, *key_ranks)


def ring(value):
    half = value.shape[0] // 2
    found = {0: value}
    up = down = value
    for step in (1, 2, 3):
        up, down = send(up, UP), send(down, DOWN)
        found[NZ - step], found[step] = up, down
    found[4] = jnp.concatenate([send(up[:half], UP), send(down[half:], DOWN)], axis=0)
    return found


def ring_sum(term, rows):
    half = rows // 2
    last = term(4)
    up = send(last[:half].astype(BF), UP).astype(F32)
    down = send(last[half:].astype(BF), DOWN).astype(F32)
    third, fifth = term(3), term(5)
    up = jnp.concatenate([third[:half] + up, third[half:]], axis=0)
    down = jnp.concatenate([fifth[:half], fifth[half:] + down], axis=0)
    for step in (2, 1, 0):
        up = send(up.astype(BF), UP).astype(F32)
        down = send(down.astype(BF), DOWN).astype(F32)
        if step:
            up, down = up + term(step), down + term(NZ - step)
    return term(0) + up + down


def own_half(value, core):
    half = value.shape[0] // 2
    return lax.dynamic_slice_in_dim(value, core * half, half, 0)


def local(
    hidden_states, route_slot, route_live, router_weight, query_weight, keyval_weight, output_weight
):
    slots = route_slot.shape[0]
    cut = slots // 2
    ctx = lax.axis_index("ctx")
    mp = lax.axis_index("mp")
    y, z, core = mp // (NZ * NC), lax.rem(mp // NC, NZ), lax.rem(mp, NC)
    place = jnp.stack([y, z, core]).astype(jnp.int32)

    first, second = gather_rows(hidden_states, route_slot, cut)

    keyval_t = keyval_weight.T
    out_q, out_kv, out_o = sibling_halves(place, query_weight, keyval_t, output_weight)
    sib_q, sib_kv, sib_o = (send(part, SIBLING) for part in (out_q, out_kv, out_o))
    weights = project_weights(place, query_weight, sib_q, keyval_t, sib_kv, router_weight)
    out_weights = output_weights(place, output_weight, sib_o)

    count = jnp.sum(route_live).astype(jnp.int32)
    counts = lax.all_gather(count.reshape(1), "ctx", axis=0, tiled=True)
    owner_ids = jnp.arange(CTX)
    starts = jnp.sum(jnp.where(owner_ids[None, :] < owner_ids[:, None], counts[None, :], 0), axis=1)

    def ranks(owner, slot):
        return jnp.where(slot < counts[owner], starts[owner] + slot, 2 * FAR)

    def dot(rows, weight):
        return jnp.dot(rows, weight, preferred_element_type=F32)

    doubled = jnp.concatenate([first, send(first, ACROSS)], axis=1)
    found_first = ring(doubled)
    found_second = ring(second)
    crossed = {e: send(value, ACROSS) for e, value in found_second.items()}

    order = (0, 1, 7, 2, 6, 3, 5, 4)
    sum_first = sum(dot(found_first[e], weights[e]) for e in order)
    sum_second = sum(
        dot(found_second[e], weights[e, :WIDTH]) + dot(crossed[e], weights[e, WIDTH:]) for e in order
    )

    queries, logits, keyvals, key_ranks = [], [], [], []
    sources = lax.rem(ctx + CTX - jnp.arange(CTX), CTX)
    for base, partial in ((0, sum_first), (cut, sum_second)):
        rows = partial.shape[0]
        other = send(partial[:, WIDTH:], SIBLING)
        queries.append((partial[:, :WIDTH] + other[:, :WIDTH]).astype(BF))
        logits.append(partial[:, 640:768] + other[:, 384:512])
        mine = own_half((partial[:, 512:640] + other[:, 256:384]).astype(BF), core)
        theirs = send(mine, PARTNER)
        even = lax.rem(z, 2) == 0
        keyval = jnp.concatenate(
            [jnp.where(even, mine, theirs), jnp.where(even, theirs, mine)], axis=1
        )
        gathered = [keyval] + [
            lax.ppermute(keyval, "ctx", [(i, (i + d) % CTX) for i in range(CTX)])
            for d in range(1, CTX)
        ]
        piece = jnp.concatenate(gathered, axis=0)
        keyvals += [piece, send(piece, SIBLING)]
        row = jnp.arange(rows // 2)
        for part in (core, 1 - core):
            slot = base + part * (rows // 2) + row
            rank = ranks(sources[:, None], slot[None, :])
            key_ranks.append(rank.reshape(1, -1))

    slot_ids = jnp.arange(slots)
    own_rank = jnp.where(slot_ids < count, starts[ctx] + slot_ids, FAR)
    own_rank = jnp.broadcast_to(own_rank[:, None], (slots, 128))
    attended = attend(own_rank, jnp.concatenate(queries, axis=0), keyvals, key_ranks, 288)

    chip = jnp.concatenate([attended, send(attended, SIBLING)], axis=1)
    chip_first, chip_second = chip[:cut], chip[cut:]

    def term_first(e):
        return dot(chip_first, out_weights[e])

    def term_second(e):
        outgoing = dot(chip_second, out_weights[e, :, WIDTH:]).astype(BF)
        return dot(chip_second, out_weights[e, :, :WIDTH]) + send(outgoing, ACROSS).astype(F32)

    total_second = ring_sum(term_second, slots - cut)
    total_first = ring_sum(term_first, cut)
    total_first = total_first[:, :WIDTH] + send(total_first[:, WIDTH:].astype(BF), ACROSS).astype(F32)

    live_slot = jnp.where(route_live == 1, route_slot, -1)
    return scatter_rows(
        hidden_states, live_slot, jnp.concatenate(logits, axis=0), total_first, total_second
    )


def solution(mesh):
    placed = (P("ctx", "mp"), P("ctx"), P("ctx"), P(), P(None, "mp"), P(None, "mp"), P("mp", None))
    return jax.shard_map(
        local, mesh=mesh, in_specs=placed, out_specs=P("ctx", "mp"), check_vma=False
    )
```

time: 375 us -> 278 us (0.74); the launches traced: 373 us -> 272 us
  waiting for transfers between devices: 237 us -> 70 us
  starting transfers between devices: 0.51 us -> 105 us
  Pallas kernels: 0 us -> 43.2 us
  blocking collectives: 41 us -> 13.2 us
  other arithmetic: 23.2 us -> 6.99 us
  matrix products: 39.8 us -> 24 us
  between operations: 13.9 us -> 1.55 us
  local copies, waits for them, and re-layouts: 17.3 us -> 7.99 us
    reduce_scatter x1 -> x0, waiting for transfers between devices: 121 us -> none  [routed_update(): lax.psum_scatter(lax.dot_general(output_weight, attended, (((0,), (1,)),...]
    all_gather x2 -> x0, waiting for transfers between devices: 109 us -> none  [the longest x1 97.5 us: routed_update(): fragment = lax.all_gather(routed_rows, 'mp', axis=1, tiled=True)]
    ppermute x2 -> x74, starting transfers between devices: 0.43 us -> 105 us  [the longest x60 77.8 us: send(): return lax.ppermute(value, 'mp', pairs)]
    ppermute x2 -> x74, waiting for transfers between devices: 7.36 us -> 70 us  [the longest x60 63.9 us: send(): return lax.ppermute(value, 'mp', pairs)]
    pallas_call x0 -> x6, Pallas kernels: none -> 43.2 us  [the longest x1 11.6 us: attend(): pl.pallas_call(attend_kernel, grid=(rows // tile, queries.shape[1] // HEA...]
    unnamed x1, blocking collectives: 41 us -> 13.2 us
    dot_general x22 -> x48, matrix products: 39.8 us -> 24 us  [dot(): return jnp.dot(rows, weight, preferred_element_type=F32)]
    scatter-add x1 -> x0, other arithmetic: 10.7 us -> none  [local(): widened = hidden_states.astype(jnp.float32).at[route_slot].add(addition)]
  transfers between devices with their start and end apart: 5 -> 74, of which waited for: 5 -> 25; matrix products, arithmetic and copies ran while one was open for 4% -> 11% of each run, Pallas kernels for 0% -> 10%
where the time goes in v1:
time: 278 us; the launch traced here: 272 us
  starting transfers between devices  105 us (38%)
  waiting for transfers between devices  70 us (25%)
  Pallas kernels  43.2 us (16%)
  matrix products  24 us (9%)
  blocking collectives  13.2 us (5%)
  local copies, waits for them, and re-layouts  7.99 us (3%)
  other arithmetic  6.99 us (3%)
    ppermute x60, starting transfers between devices, send(): return lax.ppermute(value, 'mp', pairs)  77.8 us
    ppermute x60, waiting for transfers between devices, send(): return lax.ppermute(value, 'mp', pairs)  63.9 us
    ppermute x14, starting transfers between devices, local(): lax.ppermute(keyval, 'ctx', [(i, (i + d) % CTX) for i in range(CTX)])  27.6 us
    dot_general x48, matrix products, dot(): return jnp.dot(rows, weight, preferred_element_type=F32)  24 us
    unnamed x1, blocking collectives  13.2 us
    pallas_call x1, Pallas kernels, attend(): pl.pallas_call(attend_kernel, grid=(rows // tile, queries.shape[1] // HEA...  11.6 us
    pallas_call x1, Pallas kernels, sibling_halves(): pl.pallas_call(halves_kernel, grid_spec=pltpu.PrefetchScalarGridSpec(num_...  11 us
    pallas_call x1, Pallas kernels, project_weights(): pl.pallas_call(project_weight_kernel, grid_spec=pltpu.PrefetchScalarGridS...  8.54 us
  transfers between devices with their start and end apart: 74, of which 25 were waited for; matrix products, arithmetic and copies ran while one was open for 11% of the time, Pallas kernels for 10%

profile of v1, /device:TPU:8, one launch (start us, length us, event | category | flops | bytes accessed | tf_op | source)
XLA Modules:
  0.0 272.3 jit_solution(17748667209877819017)
XLA Ops:
  1.3 11.0 %shard_map.74 = (bf16[4096,256]{1,0:T(8,128)(2,1)}, bf16[64,4096]{1,0:T(8,128)(2,1)}, bf16[256,4096]{1,0:T(8,128)(2,1)}) custom-call(s32[3]{0:T(128)S(1)} %pad_add_fusion.place_ref, bf16[8192,256]{1,0:T(8,128)(2,1)} %q1.1, bf16[64,8192]{1,0:T(8,128)(2,1)S(1)} %bitcast.216, bf16[256,8192]{1,0:T(8,128)(2,1)} %o1.1), custom_call_target="tpu_custom_call" | custom-call | bytes 9000000 | tf_op jit(solution)/shard_map/pallas_call | solution.py:122
  13.5 2.3 collective-permute-start
  15.8 4.1 %collective-permute-start.13 = (bf16[288,256]{1,0:T(8,128)(2,1)S(1)}, bf16[288,256]{1,0:T(8,128)(2,1)S(1)}, u32[]{:S(2)}, u32[]{:S(2)}) collective-permute-start(bf16[288,256]{1,0:T(8,128)(2,1)S(1)} %get-tuple-element.13), channel_id=1, source_target_pairs={{0,14},{1,15},{2,0},{3,1},{4,2},{5,3},{6,4},{7,5},{8,6},{9,7},{10,... | collective-permute-start | bytes 442376 | tf_op jit(solution)/shard_map/ppermute | solution.py:37
  20.3 1.5 collective-permute-start.4
  21.9 4.0 %collective-permute-start.3 = (bf16[288,512]{1,0:T(8,128)(2,1)S(1)}, bf16[288,512]{1,0:T(8,128)(2,1)S(1)}, u32[]{:S(2)}, u32[]{:S(2)}) collective-permute-start(bf16[288,512]{1,0:T(8,128)(2,1)S(1)} %constant_dynamic-update-slice_fusion), channel_id=1, source_target_pairs={{0,14},{1,15},{2,0},{3,1},{4,2},{5,3},{6,4},{7,5},{8,6},{9,7},{10,... | collective-permute-start | bytes 884744 | tf_op jit(solution)/shard_map/ppermute | solution.py:37
  25.9 1.9 collective-permute-start.17
  28.7 7.7 %collective-permute-done.19 = bf16[288,256]{1,0:T(8,128)(2,1)} collective-permute-done((bf16[288,256]{1,0:T(8,128)(2,1)S(1)}, bf16[288,256]{1,0:T(8,128)(2,1)}, u32[]{:S(2)}, u32[]{:S(2)}) %collective-permute-start.19) | collective-permute-done | bytes 147488 | tf_op jit(solution)/shard_map/ppermute | solution.py:37
  37.1 1.4 dynamic-update-slice
  38.5 3.3 %collective-permute-start.21 = (bf16[288,256]{1,0:T(8,128)(2,1)S(1)}, bf16[288,256]{1,0:T(8,128)(2,1)S(1)}, u32[]{:S(2)}, u32[]{:S(2)}) collective-permute-start(bf16[288,256]{1,0:T(8,128)(2,1)S(1)} %collective-permute-done.17), channel_id=1, source_target_pairs={{0,14},{1,15},{2,0},{3,1},{4,2},{5,3},{6,4},{7,5},{8,6},{9,7},{10,... | collective-permute-start | bytes 442376 | tf_op jit(solution)/shard_map/ppermute | solution.py:37
  41.9 3.3 %collective-permute-start.5 = (bf16[288,512]{1,0:T(8,128)(2,1)S(1)}, bf16[288,512]{1,0:T(8,128)(2,1)S(1)}, u32[]{:S(2)}, u32[]{:S(2)}) collective-permute-start(bf16[288,512]{1,0:T(8,128)(2,1)S(1)} %collective-permute-done.3), channel_id=1, source_target_pairs={{0,14},{1,15},{2,0},{3,1},{4,2},{5,3},{6,4},{7,5},{8,6},{9,7},{10,... | collective-permute-start | bytes 884744 | tf_op jit(solution)/shard_map/ppermute | solution.py:37
  45.1 13.2 %all-reduce = s32[8]{0:T(128)S(1)} all-reduce(s32[8]{0:T(128)S(1)} %dynamic-update-slice), channel_id=1, replica_groups=mesh['ctx'=8,'mp'=32] {'ctx'}, use_global_device_ids=true, to_apply=%add | all-reduce | flops 8 | bytes 64
  60.0 5.8 %collective-permute-done.25 = bf16[144,256]{1,0:T(8,128)(2,1)S(1)} collective-permute-done((bf16[144,256]{1,0:T(8,128)(2,1)S(1)}, bf16[144,256]{1,0:T(8,128)(2,1)S(1)}, u32[]{:S(2)}, u32[]{:S(2)}) %collective-permute-start.25) | collective-permute-done | bytes 73760 | tf_op jit(solution)/shard_map/ppermute | solution.py:37
  66.2 2.0 collective-permute-start.8
  68.3 3.0 %collective-permute-done.26 = bf16[144,256]{1,0:T(8,128)(2,1)S(1)} collective-permute-done((bf16[144,256]{1,0:T(8,128)(2,1)S(1)}, bf16[144,256]{1,0:T(8,128)(2,1)S(1)}, u32[]{:S(2)}, u32[]{:S(2)}) %collective-permute-start.26) | collective-permute-done | bytes 73760 | tf_op jit(solution)/shard_map/ppermute | solution.py:37
  71.3 1.6 collective-permute-start.12
  72.9 3.4 %collective-permute-done.7 = bf16[288,512]{1,0:T(8,128)(2,1)S(1)} collective-permute-done((bf16[288,512]{1,0:T(8,128)(2,1)S(1)}, bf16[288,512]{1,0:T(8,128)(2,1)S(1)}, u32[]{:S(2)}, u32[]{:S(2)}) %collective-permute-start.7) | collective-permute-done | bytes 294944 | tf_op jit(solution)/shard_map/ppermute | solution.py:37
  76.5 1.7 collective-permute-start.14
  78.7 1.6 collective-permute-start.18
  80.3 8.5 %shard_map.75 = bf16[8,512,768]{2,1,0:T(8,128)(2,1)} custom-call(s32[3]{0:T(128)S(1)} %pad_add_fusion.place_ref, bf16[8192,256]{1,0:T(8,128)(2,1)} %q1.1, bf16[8192,256]{1,0:T(8,128)(2,1)} %q1.1, bf16[4096,256]{1,0:T(8,128)(2,1)} %collective-permute-done.1.sq0.sq1, bf16[4096,256]{1,0:T(8,128)(2,1)} %collective-permute-done.1.sq0.sq1, ...), custom_call_target="tpu_custom_call" | custom-call | bytes 12000000 | tf_op jit(solution)/shard_map/pallas_call | solution.py:185
  89.4 1.5 fusion.33
  92.2 2.2 collective-permute-done.27
  97.7 1.7 collective-permute-start.22
  101.1 1.6 collective-permute-start.10
  107.2 8.6 %collective-permute-start.28 = (f32[288,512]{1,0:T(8,128)}, f32[288,512]{1,0:T(8,128)}, u32[]{:S(2)}, u32[]{:S(2)}) collective-permute-start(f32[288,512]{1,0:T(8,128)} %slice.373), channel_id=1, source_target_pairs={{0,1},{1,0},{2,3},{3,2},{4,5},{5,4},{6,7},{7,6},{8,9},{9,8},{10,11... | collective-permute-start | bytes 1769480 | tf_op jit(solution)/shard_map/ppermute | solution.py:37
  117.1 1.3 fusion.17
  122.6 1.3 add_select_fusion.4
  126.5 1.9 collective-permute-start.29
  129.2 2.6 collective-permute-start.39
  132.0 1.6 collective-permute-start.41
  133.6 3.0 %collective-permute-start.42 = (bf16[144,256]{1,0:T(8,128)(2,1)S(1)}, bf16[144,256]{1,0:T(8,128)(2,1)S(1)}, u32[]{:S(2)}, u32[]{:S(2)}) collective-permute-start(bf16[144,256]{1,0:T(8,128)(2,1)S(1)} %get-tuple-element.27), channel_id=1, source_target_pairs={{0,128},{32,160},{64,192},{96,224},{128,0},{160,32},{192,64},{224,... | collective-permute-start | bytes 221192 | tf_op jit(solution)/shard_map/ppermute | solution.py:368
  136.7 1.4 collective-permute-done.39
  138.0 1.8 collective-permute-start.43
  139.8 1.6 collective-permute-start.44
  141.9 3.2 %collective-permute-start.30 = (bf16[144,256]{1,0:T(8,128)(2,1)S(1)}, bf16[144,256]{1,0:T(8,128)(2,1)S(1)}, u32[]{:S(2)}, u32[]{:S(2)}) collective-permute-start(bf16[144,256]{1,0:T(8,128)(2,1)S(1)} %get-tuple-element.31), channel_id=1, source_target_pairs={{0,32},{32,64},{64,96},{96,128},{128,160},{160,192},{192,224},{224... | collective-permute-start | bytes 221192 | tf_op jit(solution)/shard_map/ppermute | solution.py:368
  145.9 3.5 %collective-permute-start.32 = (bf16[144,256]{1,0:T(8,128)(2,1)S(1)}, bf16[144,256]{1,0:T(8,128)(2,1)S(1)}, u32[]{:S(2)}, u32[]{:S(2)}) collective-permute-start(bf16[144,256]{1,0:T(8,128)(2,1)S(1)} %get-tuple-element.31), channel_id=1, source_target_pairs={{0,96},{32,128},{64,160},{96,192},{128,224},{160,0},{192,32},{224,... | collective-permute-start | bytes 221192 | tf_op jit(solution)/shard_map/ppermute | solution.py:368
  149.4 2.3 collective-permute-start.33
  151.7 4.2 %collective-permute-start.34 = (bf16[144,256]{1,0:T(8,128)(2,1)S(1)}, bf16[144,256]{1,0:T(8,128)(2,1)S(1)}, u32[]{:S(2)}, u32[]{:S(2)}) collective-permute-start(bf16[144,256]{1,0:T(8,128)(2,1)S(1)} %get-tuple-element.31), channel_id=1, source_target_pairs={{0,160},{32,192},{64,224},{96,0},{128,32},{160,64},{192,96},{224,1... | collective-permute-start | bytes 221192 | tf_op jit(solution)/shard_map/ppermute | solution.py:368
  158.6 1.8 collective-permute-done.35
  160.4 2.8 %collective-permute-done.36 = bf16[144,256]{1,0:T(8,128)(2,1)S(1)} collective-permute-done((bf16[144,256]{1,0:T(8,128)(2,1)S(1)}, bf16[144,256]{1,0:T(8,128)(2,1)S(1)}, u32[]{:S(2)}, u32[]{:S(2)}) %collective-permute-start.36) | collective-permute-done | bytes 73760 | tf_op jit(solution)/shard_map/ppermute | solution.py:368
  165.5 11.6 %shard_map.76 = bf16[576,256]{1,0:T(8,128)(2,1)S(1)} custom-call(s32[576,128]{1,0:T(8,128)S(1)} %broadcast_in_dim.32.rank_ref, bf16[576,256]{1,0:T(8,128)(2,1)S(1)} %pad_maximum_fusion.2.query_ref, bf16[1152,256]{1,0:T(8,128)(2,1)S(1)} %constant_dynamic-update-slice_fusion.4.refs_0_, bf16[1152,256]{1,0:T(8,128)(2,1)S(1)} %collective-permute-done.37.refs_1_, ...), custom_call_target="tpu_custom_call" | custom-call | flops 2717908992 | bytes 4000000 | tf_op jit(solution)/shard_map/pallas_call | solution.py:264
  177.7 6.9 %shard_map.77 = bf16[8,512,512]{2,1,0:T(8,128)(2,1)} custom-call(s32[3]{0:T(128)S(1)} %pad_add_fusion.place_ref, bf16[256,8192]{1,0:T(8,128)(2,1)} %o1.1, bf16[256,8192]{1,0:T(8,128)(2,1)} %o1.1, bf16[256,4096]{1,0:T(8,128)(2,1)S(1)} %collective-permute-done.48.so0.so1, bf16[256,4096]{1,0:T(8,128)(2,1)S(1)} %collective-permute-done.48.so0.so1), custom_call_target="tpu_custom_call" | custom-call | bytes 8000000 | tf_op jit(solution)/shard_map/pallas_call | solution.py:215
  184.6 1.3 convolution_convert_fusion.7
  191.5 1.9 collective-permute-start.59
  193.6 1.8 collective-permute-start.63
  195.7 1.8 collective-permute-start.67
  198.3 1.9 collective-permute-start.70
  201.9 9.0 %collective-permute-done.67 = bf16[288,256]{1,0:T(8,128)(2,1)S(1)} collective-permute-done((bf16[288,256]{1,0:T(8,128)(2,1)S(1)}, bf16[288,256]{1,0:T(8,128)(2,1)S(1)}, u32[]{:S(2)}, u32[]{:S(2)}) %collective-permute-start.67) | collective-permute-done | bytes 147488 | tf_op jit(solution)/shard_map/ppermute | solution.py:37
  210.9 2.6 collective-permute-start.53
  214.0 2.2 collective-permute-done.53
  216.2 3.7 %collective-permute-start.68 = (bf16[144,256]{1,0:T(8,128)(2,1)S(1)}, bf16[144,256]{1,0:T(8,128)(2,1)S(1)}, u32[]{:S(2)}, u32[]{:S(2)}) collective-permute-start(bf16[144,256]{1,0:T(8,128)(2,1)S(1)} %get-tuple-element.26), channel_id=1, source_target_pairs={{0,14},{1,15},{2,0},{3,1},{4,2},{5,3},{6,4},{7,5},{8,6},{9,7},{10,... | collective-permute-start | bytes 221192 | tf_op jit(solution)/shard_map/ppermute | solution.py:37
  220.1 1.8 collective-permute-done.68
  221.9 2.0 collective-permute-start.72
  223.9 6.6 %collective-permute-done.62 = bf16[288,256]{1,0:T(8,128)(2,1)S(1)} collective-permute-done((bf16[288,256]{1,0:T(8,128)(2,1)S(1)}, bf16[288,256]{1,0:T(8,128)(2,1)S(1)}, u32[]{:S(2)}, u32[]{:S(2)}) %collective-permute-start.62) | collective-permute-done | bytes 147488 | tf_op jit(solution)/shard_map/ppermute | solution.py:37
  231.2 6.7 %collective-permute-done.54 = bf16[288,512]{1,0:T(8,128)(2,1)S(1)} collective-permute-done((bf16[288,512]{1,0:T(8,128)(2,1)S(1)}, bf16[288,512]{1,0:T(8,128)(2,1)S(1)}, u32[]{:S(2)}, u32[]{:S(2)}) %collective-permute-start.54) | collective-permute-done | bytes 294944 | tf_op jit(solution)/shard_map/ppermute | solution.py:37
  238.3 1.9 collective-permute-start.58
  241.1 2.3 collective-permute-start.55
  243.7 3.8 %collective-permute-done.51 = bf16[288,512]{1,0:T(8,128)(2,1)S(1)} collective-permute-done((bf16[288,512]{1,0:T(8,128)(2,1)S(1)}, bf16[288,512]{1,0:T(8,128)(2,1)S(1)}, u32[]{:S(2)}, u32[]{:S(2)}) %collective-permute-start.51) | collective-permute-done | bytes 294944 | tf_op jit(solution)/shard_map/ppermute | solution.py:37
  247.8 2.3 collective-permute-done.55
  250.1 3.7 %collective-permute-start.71 = (bf16[288,256]{1,0:T(8,128)(2,1)S(1)}, bf16[288,256]{1,0:T(8,128)(2,1)S(1)}, u32[]{:S(2)}, u32[]{:S(2)}) collective-permute-start(bf16[288,256]{1,0:T(8,128)(2,1)S(1)} %add_convert_fusion.5), channel_id=1, source_target_pairs={{0,14},{1,15},{2,0},{3,1},{4,2},{5,3},{6,4},{7,5},{8,6},{9,7},{10,... | collective-permute-start | bytes 442376 | tf_op jit(solution)/shard_map/ppermute | solution.py:37
  254.4 3.2 %collective-permute-start.56 = (bf16[288,512]{1,0:T(8,128)(2,1)S(1)}, bf16[288,512]{1,0:T(8,128)(2,1)S(1)}, u32[]{:S(2)}, u32[]{:S(2)}) collective-permute-start(bf16[288,512]{1,0:T(8,128)(2,1)S(1)} %add_convert_fusion), channel_id=1, source_target_pairs={{0,14},{1,15},{2,0},{3,1},{4,2},{5,3},{6,4},{7,5},{8,6},{9,7},{10,... | collective-permute-start | bytes 884744 | tf_op jit(solution)/shard_map/ppermute | solution.py:37
  258.2 3.3 %collective-permute-start.73 = (bf16[288,256]{1,0:T(8,128)(2,1)S(1)}, bf16[288,256]{1,0:T(8,128)(2,1)S(1)}, u32[]{:S(2)}, u32[]{:S(2)}) collective-permute-start(bf16[288,256]{1,0:T(8,128)(2,1)S(1)} %add_convert_fusion.4), channel_id=1, source_target_pairs={{0,14},{1,15},{2,0},{3,1},{4,2},{5,3},{6,4},{7,5},{8,6},{9,7},{10,... | collective-permute-start | bytes 442376 | tf_op jit(solution)/shard_map/ppermute | solution.py:37
  263.0 1.3 collective-permute-done.66
  264.6 3.3 %collective-permute-done.57 = bf16[288,256]{1,0:T(8,128)(2,1)S(1)} collective-permute-done((bf16[288,256]{1,0:T(8,128)(2,1)S(1)}, bf16[288,256]{1,0:T(8,128)(2,1)S(1)}, u32[]{:S(2)}, u32[]{:S(2)}) %collective-permute-start.57) | collective-permute-done | bytes 147488 | tf_op jit(solution)/shard_map/ppermute | solution.py:37
  268.0 4.1 %shard_map.78 = bf16[3072,256]{1,0:T(8,128)(2,1)} custom-call(s32[1,576]{1,0:T(1,128)S(1)} %reshape.274.slot_ref, f32[576,128]{1,0:T(8,128)S(1)} %pad_maximum_fusion.1.gate_ref, f32[288,256]{1,0:T(8,128)S(1)} %slice_add_fusion.first_ref, f32[288,256]{1,0:T(8,128)S(1)} %fusion.13.second_ref, bf16[3072,256]{1,0:T(8,128)(2,1)S(1)} %copy-done.3), custom_call_target="tpu_custom_call" | custom-call | flops 905969664 | bytes 4000000 | tf_op jit(solution)/shard_map/pallas_call | solution.py:95
  (269 shorter events, 48.5 us)
Async XLA Ops:
  12.3 66.4 %collective-permute-start.1 = (bf16[4096,256]{1,0:T(8,128)(2,1)}, bf16[4096,256]{1,0:T(8,128)(2,1)}, u32[]{:S(2)}, u32[]{:S(2)}) collective-permute-start(bf16[4096,256]{1,0:T(8,128)(2,1)} %get-tuple-element.11), channel_id=1, source_target_pairs={{0,1},{1,0},{2,3},{3,2},{4,5},{5,4},{6,7},{7,6},{8,9},{9,8},{10,11... | collective-permute-start | bytes 6291464 | tf_op jit(solution)/shard_map/ppermute | solution.py:37
  13.5 6.8 %collective-permute-start = (bf16[288,256]{1,0:T(8,128)(2,1)S(1)}, bf16[288,256]{1,0:T(8,128)(2,1)S(1)}, u32[]{:S(2)}, u32[]{:S(2)}) collective-permute-start(bf16[288,256]{1,0:T(8,128)(2,1)S(1)} %get-tuple-element.10), channel_id=1, source_target_pairs={{0,16},{1,17},{2,18},{3,19},{4,20},{5,21},{6,22},{7,23},{8,24},{9,... | collective-permute-start | bytes 442376 | tf_op jit(solution)/shard_map/ppermute | solution.py:37
  15.8 10.1 %collective-permute-start.13 = (bf16[288,256]{1,0:T(8,128)(2,1)S(1)}, bf16[288,256]{1,0:T(8,128)(2,1)S(1)}, u32[]{:S(2)}, u32[]{:S(2)}) collective-permute-start(bf16[288,256]{1,0:T(8,128)(2,1)S(1)} %get-tuple-element.13), channel_id=1, source_target_pairs={{0,14},{1,15},{2,0},{3,1},{4,2},{5,3},{6,4},{7,5},{8,6},{9,7},{10,... | collective-permute-start | bytes 442376 | tf_op jit(solution)/shard_map/ppermute | solution.py:37
  19.9 7.9 %collective-permute-start.15 = (bf16[288,256]{1,0:T(8,128)(2,1)S(1)}, bf16[288,256]{1,0:T(8,128)(2,1)S(1)}, u32[]{:S(2)}, u32[]{:S(2)}) collective-permute-start(bf16[288,256]{1,0:T(8,128)(2,1)S(1)} %get-tuple-element.13), channel_id=1, source_target_pairs={{0,2},{1,3},{2,4},{3,5},{4,6},{5,7},{6,8},{7,9},{8,10},{9,11},{10,... | collective-permute-start | bytes 442376 | tf_op jit(solution)/shard_map/ppermute | solution.py:37
  20.3 21.5 %collective-permute-start.4 = (bf16[288,512]{1,0:T(8,128)(2,1)S(1)}, bf16[288,512]{1,0:T(8,128)(2,1)S(1)}, u32[]{:S(2)}, u32[]{:S(2)}) collective-permute-start(bf16[288,512]{1,0:T(8,128)(2,1)S(1)} %constant_dynamic-update-slice_fusion), channel_id=1, source_target_pairs={{0,2},{1,3},{2,4},{3,5},{4,6},{5,7},{6,8},{7,9},{8,10},{9,11},{10,... | collective-permute-start | bytes 884744 | tf_op jit(solution)/shard_map/ppermute | solution.py:37
  21.9 20.0 %collective-permute-start.3 = (bf16[288,512]{1,0:T(8,128)(2,1)S(1)}, bf16[288,512]{1,0:T(8,128)(2,1)S(1)}, u32[]{:S(2)}, u32[]{:S(2)}) collective-permute-start(bf16[288,512]{1,0:T(8,128)(2,1)S(1)} %constant_dynamic-update-slice_fusion), channel_id=1, source_target_pairs={{0,14},{1,15},{2,0},{3,1},{4,2},{5,3},{6,4},{7,5},{8,6},{9,7},{10,... | collective-permute-start | bytes 884744 | tf_op jit(solution)/shard_map/ppermute | solution.py:37
  25.9 12.6 %collective-permute-start.17 = (bf16[288,256]{1,0:T(8,128)(2,1)S(1)}, bf16[288,256]{1,0:T(8,128)(2,1)S(1)}, u32[]{:S(2)}, u32[]{:S(2)}) collective-permute-start(bf16[288,256]{1,0:T(8,128)(2,1)S(1)} %collective-permute-done.13), channel_id=1, source_target_pairs={{0,14},{1,15},{2,0},{3,1},{4,2},{5,3},{6,4},{7,5},{8,6},{9,7},{10,... | collective-permute-start | bytes 442376 | tf_op jit(solution)/shard_map/ppermute | solution.py:37
  27.9 8.5 %collective-permute-start.19 = (bf16[288,256]{1,0:T(8,128)(2,1)S(1)}, bf16[288,256]{1,0:T(8,128)(2,1)}, u32[]{:S(2)}, u32[]{:S(2)}) collective-permute-start(bf16[288,256]{1,0:T(8,128)(2,1)S(1)} %collective-permute-done.15), channel_id=1, source_target_pairs={{0,2},{1,3},{2,4},{3,5},{4,6},{5,7},{6,8},{7,9},{8,10},{9,11},{10,... | collective-permute-start | bytes 442376 | tf_op jit(solution)/shard_map/ppermute | solution.py:37
  36.4 22.6 %collective-permute-start.23 = (bf16[288,256]{1,0:T(8,128)(2,1)}, bf16[288,256]{1,0:T(8,128)(2,1)S(1)}, u32[]{:S(2)}, u32[]{:S(2)}) collective-permute-start(bf16[288,256]{1,0:T(8,128)(2,1)} %collective-permute-done.19), channel_id=1, source_target_pairs={{0,2},{1,3},{2,4},{3,5},{4,6},{5,7},{6,8},{7,9},{8,10},{9,11},{10,... | collective-permute-start | bytes 442376 | tf_op jit(solution)/shard_map/ppermute | solution.py:37
  38.5 21.4 %collective-permute-start.21 = (bf16[288,256]{1,0:T(8,128)(2,1)S(1)}, bf16[288,256]{1,0:T(8,128)(2,1)S(1)}, u32[]{:S(2)}, u32[]{:S(2)}) collective-permute-start(bf16[288,256]{1,0:T(8,128)(2,1)S(1)} %collective-permute-done.17), channel_id=1, source_target_pairs={{0,14},{1,15},{2,0},{3,1},{4,2},{5,3},{6,4},{7,5},{8,6},{9,7},{10,... | collective-permute-start | bytes 442376 | tf_op jit(solution)/shard_map/ppermute | solution.py:37
  41.8 24.4 %collective-permute-start.6 = (bf16[288,512]{1,0:T(8,128)(2,1)S(1)}, bf16[288,512]{1,0:T(8,128)(2,1)}, u32[]{:S(2)}, u32[]{:S(2)}) collective-permute-start(bf16[288,512]{1,0:T(8,128)(2,1)S(1)} %collective-permute-done.4), channel_id=1, source_target_pairs={{0,2},{1,3},{2,4},{3,5},{4,6},{5,7},{6,8},{7,9},{8,10},{9,11},{10,... | collective-permute-start | bytes 884744 | tf_op jit(solution)/shard_map/ppermute | solution.py:37
  41.9 24.3 %collective-permute-start.5 = (bf16[288,512]{1,0:T(8,128)(2,1)S(1)}, bf16[288,512]{1,0:T(8,128)(2,1)S(1)}, u32[]{:S(2)}, u32[]{:S(2)}) collective-permute-start(bf16[288,512]{1,0:T(8,128)(2,1)S(1)} %collective-permute-done.3), channel_id=1, source_target_pairs={{0,14},{1,15},{2,0},{3,1},{4,2},{5,3},{6,4},{7,5},{8,6},{9,7},{10,... | collective-permute-start | bytes 884744 | tf_op jit(solution)/shard_map/ppermute | solution.py:37
  59.0 19.1 %collective-permute-start.2 = (bf16[64,4096]{1,0:T(8,128)(2,1)}, bf16[64,4096]{1,0:T(8,128)(2,1)}, u32[]{:S(2)}, u32[]{:S(2)}) collective-permute-start(bf16[64,4096]{1,0:T(8,128)(2,1)} %get-tuple-element.12), channel_id=1, source_target_pairs={{0,1},{1,0},{2,3},{3,2},{4,5},{5,4},{6,7},{7,6},{8,9},{9,8},{10,11... | collective-permute-start | bytes 1572872 | tf_op jit(solution)/shard_map/ppermute | solution.py:37
  59.9 6.0 %collective-permute-start.25 = (bf16[144,256]{1,0:T(8,128)(2,1)S(1)}, bf16[144,256]{1,0:T(8,128)(2,1)S(1)}, u32[]{:S(2)}, u32[]{:S(2)}) collective-permute-start(bf16[144,256]{1,0:T(8,128)(2,1)S(1)} %slice.368), channel_id=1, source_target_pairs={{0,2},{1,3},{2,4},{3,5},{4,6},{5,7},{6,8},{7,9},{8,10},{9,11},{10,... | collective-permute-start | bytes 221192 | tf_op jit(solution)/shard_map/ppermute | solution.py:37
  66.1 10.2 %collective-permute-start.7 = (bf16[288,512]{1,0:T(8,128)(2,1)S(1)}, bf16[288,512]{1,0:T(8,128)(2,1)S(1)}, u32[]{:S(2)}, u32[]{:S(2)}) collective-permute-start(bf16[288,512]{1,0:T(8,128)(2,1)S(1)} %collective-permute-done.5), channel_id=1, source_target_pairs={{0,14},{1,15},{2,0},{3,1},{4,2},{5,3},{6,4},{7,5},{8,6},{9,7},{10,... | collective-permute-start | bytes 884744 | tf_op jit(solution)/shard_map/ppermute | solution.py:37
  66.2 10.2 %collective-permute-start.8 = (bf16[288,512]{1,0:T(8,128)(2,1)}, bf16[288,512]{1,0:T(8,128)(2,1)S(1)}, u32[]{:S(2)}, u32[]{:S(2)}) collective-permute-start(bf16[288,512]{1,0:T(8,128)(2,1)} %collective-permute-done.6), channel_id=1, source_target_pairs={{0,2},{1,3},{2,4},{3,5},{4,6},{5,7},{6,8},{7,9},{8,10},{9,11},{10,... | collective-permute-start | bytes 884744 | tf_op jit(solution)/shard_map/ppermute | solution.py:37
  71.3 17.6 %collective-permute-start.12 = (bf16[288,256]{1,0:T(8,128)(2,1)S(1)}, bf16[288,256]{1,0:T(8,128)(2,1)S(1)}, u32[]{:S(2)}, u32[]{:S(2)}) collective-permute-start(bf16[288,256]{1,0:T(8,128)(2,1)S(1)} %get-tuple-element.13), channel_id=1, source_target_pairs={{0,16},{1,17},{2,18},{3,19},{4,20},{5,21},{6,22},{7,23},{8,24},{9,... | collective-permute-start | bytes 442376 | tf_op jit(solution)/shard_map/ppermute | solution.py:37
  76.4 101.3 %collective-permute-start.48 = (bf16[256,4096]{1,0:T(8,128)(2,1)}, bf16[256,4096]{1,0:T(8,128)(2,1)S(1)}, u32[]{:S(2)}, u32[]{:S(2)}) collective-permute-start(bf16[256,4096]{1,0:T(8,128)(2,1)} %get-tuple-element.14), channel_id=1, source_target_pairs={{0,1},{1,0},{2,3},{3,2},{4,5},{5,4},{6,7},{7,6},{8,9},{9,8},{10,11... | collective-permute-start | bytes 6291464 | tf_op jit(solution)/shard_map/ppermute | solution.py:37
  76.5 21.2 %collective-permute-start.14 = (bf16[288,256]{1,0:T(8,128)(2,1)}, bf16[288,256]{1,0:T(8,128)(2,1)S(1)}, u32[]{:S(2)}, u32[]{:S(2)}) collective-permute-start(bf16[288,256]{1,0:T(8,128)(2,1)} %copy-done.19), channel_id=1, source_target_pairs={{0,16},{1,17},{2,18},{3,19},{4,20},{5,21},{6,22},{7,23},{8,24},{9,... | collective-permute-start | bytes 442376 | tf_op jit(solution)/shard_map/ppermute | solution.py:37
  78.2 21.8 %collective-permute-start.16 = (bf16[288,256]{1,0:T(8,128)(2,1)}, bf16[288,256]{1,0:T(8,128)(2,1)S(1)}, u32[]{:S(2)}, u32[]{:S(2)}) collective-permute-start(bf16[288,256]{1,0:T(8,128)(2,1)} %copy-done.17), channel_id=1, source_target_pairs={{0,16},{1,17},{2,18},{3,19},{4,20},{5,21},{6,22},{7,23},{8,24},{9,... | collective-permute-start | bytes 442376 | tf_op jit(solution)/shard_map/ppermute | solution.py:37
  78.7 22.4 %collective-permute-start.18 = (bf16[288,256]{1,0:T(8,128)(2,1)}, bf16[288,256]{1,0:T(8,128)(2,1)S(1)}, u32[]{:S(2)}, u32[]{:S(2)}) collective-permute-start(bf16[288,256]{1,0:T(8,128)(2,1)} %copy-done.21), channel_id=1, source_target_pairs={{0,16},{1,17},{2,18},{3,19},{4,20},{5,21},{6,22},{7,23},{8,24},{9,... | collective-permute-start | bytes 442376 | tf_op jit(solution)/shard_map/ppermute | solution.py:37
  94.4 9.8 %collective-permute-start.20 = (bf16[288,256]{1,0:T(8,128)(2,1)}, bf16[288,256]{1,0:T(8,128)(2,1)S(1)}, u32[]{:S(2)}, u32[]{:S(2)}) collective-permute-start(bf16[288,256]{1,0:T(8,128)(2,1)} %collective-permute-done.19), channel_id=1, source_target_pairs={{0,16},{1,17},{2,18},{3,19},{4,20},{5,21},{6,22},{7,23},{8,24},{9,... | collective-permute-start | bytes 442376 | tf_op jit(solution)/shard_map/ppermute | solution.py:37
  97.7 7.6 %collective-permute-start.22 = (bf16[288,256]{1,0:T(8,128)(2,1)S(1)}, bf16[288,256]{1,0:T(8,128)(2,1)S(1)}, u32[]{:S(2)}, u32[]{:S(2)}) collective-permute-start(bf16[288,256]{1,0:T(8,128)(2,1)S(1)} %copy-done.10), channel_id=1, source_target_pairs={{0,16},{1,17},{2,18},{3,19},{4,20},{5,21},{6,22},{7,23},{8,24},{9,... | collective-permute-start | bytes 442376 | tf_op jit(solution)/shard_map/ppermute | solution.py:37
  100.0 6.1 %collective-permute-start.24 = (bf16[288,256]{1,0:T(8,128)(2,1)S(1)}, bf16[288,256]{1,0:T(8,128)(2,1)S(1)}, u32[]{:S(2)}, u32[]{:S(2)}) collective-permute-start(bf16[288,256]{1,0:T(8,128)(2,1)S(1)} %collective-permute-done.23), channel_id=1, source_target_pairs={{0,16},{1,17},{2,18},{3,19},{4,20},{5,21},{6,22},{7,23},{8,24},{9,... | collective-permute-start | bytes 442376 | tf_op jit(solution)/shard_map/ppermute | solution.py:37
  101.1 18.1 %collective-permute-start.10 = (bf16[144,512]{1,0:T(8,128)(2,1)S(1)}, bf16[144,512]{1,0:T(8,128)(2,1)S(1)}, u32[]{:S(2)}, u32[]{:S(2)}) collective-permute-start(bf16[144,512]{1,0:T(8,128)(2,1)S(1)} %slice.349), channel_id=1, source_target_pairs={{0,14},{1,15},{2,0},{3,1},{4,2},{5,3},{6,4},{7,5},{8,6},{9,7},{10,... | collective-permute-start | bytes 442376 | tf_op jit(solution)/shard_map/ppermute | solution.py:37
  104.1 15.1 %collective-permute-start.9 = (bf16[144,512]{1,0:T(8,128)(2,1)S(1)}, bf16[144,512]{1,0:T(8,128)(2,1)S(1)}, u32[]{:S(2)}, u32[]{:S(2)}) collective-permute-start(bf16[144,512]{1,0:T(8,128)(2,1)S(1)} %slice.348), channel_id=1, source_target_pairs={{0,2},{1,3},{2,4},{3,5},{4,6},{5,7},{6,8},{7,9},{8,10},{9,11},{10,... | collective-permute-start | bytes 442376 | tf_op jit(solution)/shard_map/ppermute | solution.py:37
  107.2 16.7 %collective-permute-start.28 = (f32[288,512]{1,0:T(8,128)}, f32[288,512]{1,0:T(8,128)}, u32[]{:S(2)}, u32[]{:S(2)}) collective-permute-start(f32[288,512]{1,0:T(8,128)} %slice.373), channel_id=1, source_target_pairs={{0,1},{1,0},{2,3},{3,2},{4,5},{5,4},{6,7},{7,6},{8,9},{9,8},{10,11... | collective-permute-start | bytes 1769480 | tf_op jit(solution)/shard_map/ppermute | solution.py:37
  126.5 7.1 %collective-permute-start.29 = (bf16[144,128]{1,0:T(8,128)(2,1)S(1)}, bf16[144,128]{1,0:T(8,128)(2,1)S(1)}, u32[]{:S(2)}, u32[]{:S(2)}) collective-permute-start(bf16[144,128]{1,0:T(8,128)(2,1)S(1)} %fusion.45), channel_id=1, source_target_pairs={{0,2},{1,3},{2,0},{3,1},{4,6},{5,7},{6,4},{7,5},{8,10},{9,11},{10,... | collective-permute-start | bytes 110600 | tf_op jit(solution)/shard_map/ppermute | solution.py:37
  129.2 8.8 %collective-permute-start.39 = (bf16[144,256]{1,0:T(8,128)(2,1)S(1)}, bf16[144,256]{1,0:T(8,128)(2,1)S(1)}, u32[]{:S(2)}, u32[]{:S(2)}) collective-permute-start(bf16[144,256]{1,0:T(8,128)(2,1)S(1)} %get-tuple-element.27), channel_id=1, source_target_pairs={{0,32},{32,64},{64,96},{96,128},{128,160},{160,192},{192,224},{224... | collective-permute-start | bytes 221192 | tf_op jit(solution)/shard_map/ppermute | solution.py:368
  131.8 8.0 %collective-permute-start.40 = (bf16[144,256]{1,0:T(8,128)(2,1)S(1)}, bf16[144,256]{1,0:T(8,128)(2,1)S(1)}, u32[]{:S(2)}, u32[]{:S(2)}) collective-permute-start(bf16[144,256]{1,0:T(8,128)(2,1)S(1)} %get-tuple-element.27), channel_id=1, source_target_pairs={{0,64},{32,96},{64,128},{96,160},{128,192},{160,224},{192,0},{224,... | collective-permute-start | bytes 221192 | tf_op jit(solution)/shard_map/ppermute | solution.py:368
  132.0 9.4 %collective-permute-start.41 = (bf16[144,256]{1,0:T(8,128)(2,1)S(1)}, bf16[144,256]{1,0:T(8,128)(2,1)S(1)}, u32[]{:S(2)}, u32[]{:S(2)}) collective-permute-start(bf16[144,256]{1,0:T(8,128)(2,1)S(1)} %get-tuple-element.27), channel_id=1, source_target_pairs={{0,96},{32,128},{64,160},{96,192},{128,224},{160,0},{192,32},{224,... | collective-permute-start | bytes 221192 | tf_op jit(solution)/shard_map/ppermute | solution.py:368
  133.6 8.3 %collective-permute-start.42 = (bf16[144,256]{1,0:T(8,128)(2,1)S(1)}, bf16[144,256]{1,0:T(8,128)(2,1)S(1)}, u32[]{:S(2)}, u32[]{:S(2)}) collective-permute-start(bf16[144,256]{1,0:T(8,128)(2,1)S(1)} %get-tuple-element.27), channel_id=1, source_target_pairs={{0,128},{32,160},{64,192},{96,224},{128,0},{160,32},{192,64},{224,... | collective-permute-start | bytes 221192 | tf_op jit(solution)/shard_map/ppermute | solution.py:368
  138.0 7.0 %collective-permute-start.43 = (bf16[144,256]{1,0:T(8,128)(2,1)S(1)}, bf16[144,256]{1,0:T(8,128)(2,1)S(1)}, u32[]{:S(2)}, u32[]{:S(2)}) collective-permute-start(bf16[144,256]{1,0:T(8,128)(2,1)S(1)} %get-tuple-element.27), channel_id=1, source_target_pairs={{0,160},{32,192},{64,224},{96,0},{128,32},{160,64},{192,96},{224,1... | collective-permute-start | bytes 221192 | tf_op jit(solution)/shard_map/ppermute | solution.py:368
  139.8 6.1 %collective-permute-start.44 = (bf16[144,256]{1,0:T(8,128)(2,1)S(1)}, bf16[144,256]{1,0:T(8,128)(2,1)S(1)}, u32[]{:S(2)}, u32[]{:S(2)}) collective-permute-start(bf16[144,256]{1,0:T(8,128)(2,1)S(1)} %get-tuple-element.27), channel_id=1, source_target_pairs={{0,192},{32,224},{64,0},{96,32},{128,64},{160,96},{192,128},{224,1... | collective-permute-start | bytes 221192 | tf_op jit(solution)/shard_map/ppermute | solution.py:368
  141.4 8.0 %collective-permute-start.45 = (bf16[144,256]{1,0:T(8,128)(2,1)S(1)}, bf16[144,256]{1,0:T(8,128)(2,1)S(1)}, u32[]{:S(2)}, u32[]{:S(2)}) collective-permute-start(bf16[144,256]{1,0:T(8,128)(2,1)S(1)} %get-tuple-element.27), channel_id=1, source_target_pairs={{0,224},{32,0},{64,32},{96,64},{128,96},{160,128},{192,160},{224,1... | collective-permute-start | bytes 221192 | tf_op jit(solution)/shard_map/ppermute | solution.py:368
  141.9 9.8 %collective-permute-start.30 = (bf16[144,256]{1,0:T(8,128)(2,1)S(1)}, bf16[144,256]{1,0:T(8,128)(2,1)S(1)}, u32[]{:S(2)}, u32[]{:S(2)}) collective-permute-start(bf16[144,256]{1,0:T(8,128)(2,1)S(1)} %get-tuple-element.31), channel_id=1, source_target_pairs={{0,32},{32,64},{64,96},{96,128},{128,160},{160,192},{192,224},{224... | collective-permute-start | bytes 221192 | tf_op jit(solution)/shard_map/ppermute | solution.py:368
  145.1 10.8 %collective-permute-start.31 = (bf16[144,256]{1,0:T(8,128)(2,1)S(1)}, bf16[144,256]{1,0:T(8,128)(2,1)S(1)}, u32[]{:S(2)}, u32[]{:S(2)}) collective-permute-start(bf16[144,256]{1,0:T(8,128)(2,1)S(1)} %get-tuple-element.31), channel_id=1, source_target_pairs={{0,64},{32,96},{64,128},{96,160},{128,192},{160,224},{192,0},{224,... | collective-permute-start | bytes 221192 | tf_op jit(solution)/shard_map/ppermute | solution.py:368
  145.9 11.4 %collective-permute-start.32 = (bf16[144,256]{1,0:T(8,128)(2,1)S(1)}, bf16[144,256]{1,0:T(8,128)(2,1)S(1)}, u32[]{:S(2)}, u32[]{:S(2)}) collective-permute-start(bf16[144,256]{1,0:T(8,128)(2,1)S(1)} %get-tuple-element.31), channel_id=1, source_target_pairs={{0,96},{32,128},{64,160},{96,192},{128,224},{160,0},{192,32},{224,... | collective-permute-start | bytes 221192 | tf_op jit(solution)/shard_map/ppermute | solution.py:368
  149.4 9.0 %collective-permute-start.33 = (bf16[144,256]{1,0:T(8,128)(2,1)S(1)}, bf16[144,256]{1,0:T(8,128)(2,1)S(1)}, u32[]{:S(2)}, u32[]{:S(2)}) collective-permute-start(bf16[144,256]{1,0:T(8,128)(2,1)S(1)} %get-tuple-element.31), channel_id=1, source_target_pairs={{0,128},{32,160},{64,192},{96,224},{128,0},{160,32},{192,64},{224,... | collective-permute-start | bytes 221192 | tf_op jit(solution)/shard_map/ppermute | solution.py:368
  151.7 6.8 %collective-permute-start.34 = (bf16[144,256]{1,0:T(8,128)(2,1)S(1)}, bf16[144,256]{1,0:T(8,128)(2,1)S(1)}, u32[]{:S(2)}, u32[]{:S(2)}) collective-permute-start(bf16[144,256]{1,0:T(8,128)(2,1)S(1)} %get-tuple-element.31), channel_id=1, source_target_pairs={{0,160},{32,192},{64,224},{96,0},{128,32},{160,64},{192,96},{224,1... | collective-permute-start | bytes 221192 | tf_op jit(solution)/shard_map/ppermute | solution.py:368
  158.4 7.0 %collective-permute-start.46 = (bf16[1152,256]{1,0:T(8,128)(2,1)S(1)}, bf16[1152,256]{1,0:T(8,128)(2,1)S(1)}, u32[]{:S(2)}, u32[]{:S(2)}) collective-permute-start(bf16[1152,256]{1,0:T(8,128)(2,1)S(1)} %constant_dynamic-update-slice_fusion.12.refs_2_), channel_id=1, source_target_pairs={{0,1},{1,0},{2,3},{3,2},{4,5},{5,4},{6,7},{7,6},{8,9},{9,8},{10,11... | collective-permute-start | bytes 1769480 | tf_op jit(solution)/shard_map/ppermute | solution.py:37
  177.1 7.5 %collective-permute-start.47 = (bf16[576,256]{1,0:T(8,128)(2,1)S(1)}, bf16[576,256]{1,0:T(8,128)(2,1)S(1)}, u32[]{:S(2)}, u32[]{:S(2)}) collective-permute-start(bf16[576,256]{1,0:T(8,128)(2,1)S(1)} %shard_map.76), channel_id=1, source_target_pairs={{0,1},{1,0},{2,3},{3,2},{4,5},{5,4},{6,7},{7,6},{8,9},{9,8},{10,11... | collective-permute-start | bytes 884744 | tf_op jit(solution)/shard_map/ppermute | solution.py:37
  191.5 6.8 %collective-permute-start.59 = (bf16[288,256]{1,0:T(8,128)(2,1)S(1)}, bf16[288,256]{1,0:T(8,128)(2,1)S(1)}, u32[]{:S(2)}, u32[]{:S(2)}) collective-permute-start(bf16[288,256]{1,0:T(8,128)(2,1)S(1)} %convolution_convert_fusion.7), channel_id=1, source_target_pairs={{0,16},{1,17},{2,18},{3,19},{4,20},{5,21},{6,22},{7,23},{8,24},{9,... | collective-permute-start | bytes 442376 | tf_op jit(solution)/shard_map/ppermute | solution.py:37
  193.4 8.1 %collective-permute-start.60 = (bf16[288,256]{1,0:T(8,128)(2,1)S(1)}, bf16[288,256]{1,0:T(8,128)(2,1)S(1)}, u32[]{:S(2)}, u32[]{:S(2)}) collective-permute-start(bf16[288,256]{1,0:T(8,128)(2,1)S(1)} %convolution_convert_fusion.6), channel_id=1, source_target_pairs={{0,16},{1,17},{2,18},{3,19},{4,20},{5,21},{6,22},{7,23},{8,24},{9,... | collective-permute-start | bytes 442376 | tf_op jit(solution)/shard_map/ppermute | solution.py:37
  193.6 28.3 %collective-permute-start.63 = (bf16[288,256]{1,0:T(8,128)(2,1)S(1)}, bf16[288,256]{1,0:T(8,128)(2,1)S(1)}, u32[]{:S(2)}, u32[]{:S(2)}) collective-permute-start(bf16[288,256]{1,0:T(8,128)(2,1)S(1)} %convolution_convert_fusion.5), channel_id=1, source_target_pairs={{0,16},{1,17},{2,18},{3,19},{4,20},{5,21},{6,22},{7,23},{8,24},{9,... | collective-permute-start | bytes 442376 | tf_op jit(solution)/shard_map/ppermute | solution.py:37
  195.4 58.7 %collective-permute-start.65 = (bf16[288,256]{1,0:T(8,128)(2,1)S(1)}, bf16[288,256]{1,0:T(8,128)(2,1)S(1)}, u32[]{:S(2)}, u32[]{:S(2)}) collective-permute-start(bf16[288,256]{1,0:T(8,128)(2,1)S(1)} %convolution_convert_fusion.4), channel_id=1, source_target_pairs={{0,16},{1,17},{2,18},{3,19},{4,20},{5,21},{6,22},{7,23},{8,24},{9,... | collective-permute-start | bytes 442376 | tf_op jit(solution)/shard_map/ppermute | solution.py:37
  195.7 15.3 %collective-permute-start.67 = (bf16[288,256]{1,0:T(8,128)(2,1)S(1)}, bf16[288,256]{1,0:T(8,128)(2,1)S(1)}, u32[]{:S(2)}, u32[]{:S(2)}) collective-permute-start(bf16[288,256]{1,0:T(8,128)(2,1)S(1)} %convolution_convert_fusion.3), channel_id=1, source_target_pairs={{0,16},{1,17},{2,18},{3,19},{4,20},{5,21},{6,22},{7,23},{8,24},{9,... | collective-permute-start | bytes 442376 | tf_op jit(solution)/shard_map/ppermute | solution.py:37
  198.3 40.0 %collective-permute-start.70 = (bf16[288,256]{1,0:T(8,128)(2,1)S(1)}, bf16[288,256]{1,0:T(8,128)(2,1)S(1)}, u32[]{:S(2)}, u32[]{:S(2)}) collective-permute-start(bf16[288,256]{1,0:T(8,128)(2,1)S(1)} %convolution_convert_fusion.2), channel_id=1, source_target_pairs={{0,16},{1,17},{2,18},{3,19},{4,20},{5,21},{6,22},{7,23},{8,24},{9,... | collective-permute-start | bytes 442376 | tf_op jit(solution)/shard_map/ppermute | solution.py:37
  201.5 12.3 %collective-permute-start.49 = (bf16[144,512]{1,0:T(8,128)(2,1)S(1)}, bf16[144,512]{1,0:T(8,128)(2,1)S(1)}, u32[]{:S(2)}, u32[]{:S(2)}) collective-permute-start(bf16[144,512]{1,0:T(8,128)(2,1)S(1)} %get-tuple-element.23), channel_id=1, source_target_pairs={{0,2},{1,3},{2,4},{3,5},{4,6},{5,7},{6,8},{7,9},{8,10},{9,11},{10,... | collective-permute-start | bytes 442376 | tf_op jit(solution)/shard_map/ppermute | solution.py:37
  213.8 6.2 %collective-permute-start.61 = (bf16[144,256]{1,0:T(8,128)(2,1)S(1)}, bf16[144,256]{1,0:T(8,128)(2,1)S(1)}, u32[]{:S(2)}, u32[]{:S(2)}) collective-permute-start(bf16[144,256]{1,0:T(8,128)(2,1)S(1)} %get-tuple-element.25), channel_id=1, source_target_pairs={{0,2},{1,3},{2,4},{3,5},{4,6},{5,7},{6,8},{7,9},{8,10},{9,11},{10,... | collective-permute-start | bytes 221192 | tf_op jit(solution)/shard_map/ppermute | solution.py:37
  219.9 10.9 %collective-permute-start.50 = (bf16[288,512]{1,0:T(8,128)(2,1)S(1)}, bf16[288,512]{1,0:T(8,128)(2,1)S(1)}, u32[]{:S(2)}, u32[]{:S(2)}) collective-permute-start(bf16[288,512]{1,0:T(8,128)(2,1)S(1)} %pad_maximum_fusion.3), channel_id=1, source_target_pairs={{0,2},{1,3},{2,4},{3,5},{4,6},{5,7},{6,8},{7,9},{8,10},{9,11},{10,... | collective-permute-start | bytes 884744 | tf_op jit(solution)/shard_map/ppermute | solution.py:37
  221.8 8.6 %collective-permute-start.62 = (bf16[288,256]{1,0:T(8,128)(2,1)S(1)}, bf16[288,256]{1,0:T(8,128)(2,1)S(1)}, u32[]{:S(2)}, u32[]{:S(2)}) collective-permute-start(bf16[288,256]{1,0:T(8,128)(2,1)S(1)} %pad_maximum_fusion.5), channel_id=1, source_target_pairs={{0,2},{1,3},{2,4},{3,5},{4,6},{5,7},{6,8},{7,9},{8,10},{9,11},{10,... | collective-permute-start | bytes 442376 | tf_op jit(solution)/shard_map/ppermute | solution.py:37
  221.9 36.0 %collective-permute-start.72 = (bf16[288,256]{1,0:T(8,128)(2,1)S(1)}, bf16[288,256]{1,0:T(8,128)(2,1)S(1)}, u32[]{:S(2)}, u32[]{:S(2)}) collective-permute-start(bf16[288,256]{1,0:T(8,128)(2,1)S(1)} %convolution_convert_fusion.1), channel_id=1, source_target_pairs={{0,16},{1,17},{2,18},{3,19},{4,20},{5,21},{6,22},{7,23},{8,24},{9,... | collective-permute-start | bytes 442376 | tf_op jit(solution)/shard_map/ppermute | solution.py:37
  230.5 7.4 %collective-permute-start.54 = (bf16[288,512]{1,0:T(8,128)(2,1)S(1)}, bf16[288,512]{1,0:T(8,128)(2,1)S(1)}, u32[]{:S(2)}, u32[]{:S(2)}) collective-permute-start(bf16[288,512]{1,0:T(8,128)(2,1)S(1)} %pad_maximum_fusion.4), channel_id=1, source_target_pairs={{0,14},{1,15},{2,0},{3,1},{4,2},{5,3},{6,4},{7,5},{8,6},{9,7},{10,... | collective-permute-start | bytes 884744 | tf_op jit(solution)/shard_map/ppermute | solution.py:37
  230.8 10.3 %collective-permute-start.69 = (bf16[288,256]{1,0:T(8,128)(2,1)S(1)}, bf16[288,256]{1,0:T(8,128)(2,1)S(1)}, u32[]{:S(2)}, u32[]{:S(2)}) collective-permute-start(bf16[288,256]{1,0:T(8,128)(2,1)S(1)} %pad_maximum_fusion.6), channel_id=1, source_target_pairs={{0,14},{1,15},{2,0},{3,1},{4,2},{5,3},{6,4},{7,5},{8,6},{9,7},{10,... | collective-permute-start | bytes 442376 | tf_op jit(solution)/shard_map/ppermute | solution.py:37
  237.9 9.5 %collective-permute-start.51 = (bf16[288,512]{1,0:T(8,128)(2,1)S(1)}, bf16[288,512]{1,0:T(8,128)(2,1)S(1)}, u32[]{:S(2)}, u32[]{:S(2)}) collective-permute-start(bf16[288,512]{1,0:T(8,128)(2,1)S(1)} %add_convert_fusion.3), channel_id=1, source_target_pairs={{0,2},{1,3},{2,4},{3,5},{4,6},{5,7},{6,8},{7,9},{8,10},{9,11},{10,... | collective-permute-start | bytes 884744 | tf_op jit(solution)/shard_map/ppermute | solution.py:37
  238.3 24.7 %collective-permute-start.58 = (bf16[288,256]{1,0:T(8,128)(2,1)S(1)}, bf16[288,256]{1,0:T(8,128)(2,1)S(1)}, u32[]{:S(2)}, u32[]{:S(2)}) collective-permute-start(bf16[288,256]{1,0:T(8,128)(2,1)S(1)} %convolution_convert_fusion.8), channel_id=1, source_target_pairs={{0,16},{1,17},{2,18},{3,19},{4,20},{5,21},{6,22},{7,23},{8,24},{9,... | collective-permute-start | bytes 442376 | tf_op jit(solution)/shard_map/ppermute | solution.py:37
  241.1 9.0 %collective-permute-start.55 = (bf16[288,512]{1,0:T(8,128)(2,1)S(1)}, bf16[288,512]{1,0:T(8,128)(2,1)S(1)}, u32[]{:S(2)}, u32[]{:S(2)}) collective-permute-start(bf16[288,512]{1,0:T(8,128)(2,1)S(1)} %add_convert_fusion.1), channel_id=1, source_target_pairs={{0,14},{1,15},{2,0},{3,1},{4,2},{5,3},{6,4},{7,5},{8,6},{9,7},{10,... | collective-permute-start | bytes 884744 | tf_op jit(solution)/shard_map/ppermute | solution.py:37
  247.4 7.0 %collective-permute-start.64 = (bf16[288,256]{1,0:T(8,128)(2,1)S(1)}, bf16[288,256]{1,0:T(8,128)(2,1)S(1)}, u32[]{:S(2)}, u32[]{:S(2)}) collective-permute-start(bf16[288,256]{1,0:T(8,128)(2,1)S(1)} %add_convert_fusion.7), channel_id=1, source_target_pairs={{0,2},{1,3},{2,4},{3,5},{4,6},{5,7},{6,8},{7,9},{8,10},{9,11},{10,... | collective-permute-start | bytes 442376 | tf_op jit(solution)/shard_map/ppermute | solution.py:37
  250.1 7.9 %collective-permute-start.71 = (bf16[288,256]{1,0:T(8,128)(2,1)S(1)}, bf16[288,256]{1,0:T(8,128)(2,1)S(1)}, u32[]{:S(2)}, u32[]{:S(2)}) collective-permute-start(bf16[288,256]{1,0:T(8,128)(2,1)S(1)} %add_convert_fusion.5), channel_id=1, source_target_pairs={{0,14},{1,15},{2,0},{3,1},{4,2},{5,3},{6,4},{7,5},{8,6},{9,7},{10,... | collective-permute-start | bytes 442376 | tf_op jit(solution)/shard_map/ppermute | solution.py:37
  254.1 8.2 %collective-permute-start.52 = (bf16[288,512]{1,0:T(8,128)(2,1)S(1)}, bf16[288,512]{1,0:T(8,128)(2,1)S(1)}, u32[]{:S(2)}, u32[]{:S(2)}) collective-permute-start(bf16[288,512]{1,0:T(8,128)(2,1)S(1)} %add_convert_fusion.2), channel_id=1, source_target_pairs={{0,2},{1,3},{2,4},{3,5},{4,6},{5,7},{6,8},{7,9},{8,10},{9,11},{10,... | collective-permute-start | bytes 884744 | tf_op jit(solution)/shard_map/ppermute | solution.py:37
  254.4 7.9 %collective-permute-start.56 = (bf16[288,512]{1,0:T(8,128)(2,1)S(1)}, bf16[288,512]{1,0:T(8,128)(2,1)S(1)}, u32[]{:S(2)}, u32[]{:S(2)}) collective-permute-start(bf16[288,512]{1,0:T(8,128)(2,1)S(1)} %add_convert_fusion), channel_id=1, source_target_pairs={{0,14},{1,15},{2,0},{3,1},{4,2},{5,3},{6,4},{7,5},{8,6},{9,7},{10,... | collective-permute-start | bytes 884744 | tf_op jit(solution)/shard_map/ppermute | solution.py:37
  257.9 6.4 %collective-permute-start.66 = (bf16[288,256]{1,0:T(8,128)(2,1)S(1)}, bf16[288,256]{1,0:T(8,128)(2,1)S(1)}, u32[]{:S(2)}, u32[]{:S(2)}) collective-permute-start(bf16[288,256]{1,0:T(8,128)(2,1)S(1)} %add_convert_fusion.6), channel_id=1, source_target_pairs={{0,2},{1,3},{2,4},{3,5},{4,6},{5,7},{6,8},{7,9},{8,10},{9,11},{10,... | collective-permute-start | bytes 442376 | tf_op jit(solution)/shard_map/ppermute | solution.py:37
  258.2 6.1 %collective-permute-start.73 = (bf16[288,256]{1,0:T(8,128)(2,1)S(1)}, bf16[288,256]{1,0:T(8,128)(2,1)S(1)}, u32[]{:S(2)}, u32[]{:S(2)}) collective-permute-start(bf16[288,256]{1,0:T(8,128)(2,1)S(1)} %add_convert_fusion.4), channel_id=1, source_target_pairs={{0,14},{1,15},{2,0},{3,1},{4,2},{5,3},{6,4},{7,5},{8,6},{9,7},{10,... | collective-permute-start | bytes 442376 | tf_op jit(solution)/shard_map/ppermute | solution.py:37
  (37 other events, 571.3 us)
